TPU v7x, 32 devices: a whole 2x2x4 slice. The times are simulated.
32 devices in a mesh: energy: 8 (over y, x, core), space: 4 (over z).
Axes of the slice: x: 2, y: 2, z: 4, core: 2. Of those that a mesh axis runs over, the one named last changes fastest.
Arguments:
- green: bfloat16 [4, 8, 4, 384, 384], P(None, 'energy', 'space'), may hold values from -6 to 6
- v_diag: bfloat16 [4, 384, 384], P('space'), may hold values from -0.3125 to 0.3125
- v_low: bfloat16 [4, 384, 384], P('space'), may hold values from -0.3125 to 0.3125
- energy_slot: int32 [8], replicated, may hold values from 0 to 7, each once
Outputs:
- sigma: bfloat16 [2, 8, 4, 384, 384], P(None, None, 'space', 'energy')
Inputs may be any that keep to these rules, and one draw needn't show every extreme that they name: `energy_slot`: each grid energy appears in exactly one slot.
All inputs are finite; a program needn't handle non-finite values.
Results may differ from a plain program's by a relative error of at most 0.0066.
Values may be sent and summed in bfloat16 or wider, within the bound.
No kernel may reach another device: no remote copies, remote signals or barrier semaphores. Data moves between devices by JAX's collectives and lax.ppermute only.
A program may use at most 64 MiB of HBM per device.

v0:
```python
import math
import jax
import jax.numpy as jnp
from jax import lax
from jax.sharding import PartitionSpec as P


def shifted(value, axis, steps):
    count = lax.axis_size(axis)
    leading, last = (max(0, -steps), min(count, count - steps))
    return lax.ppermute(value, axis, [(source, source + steps) for source in range(leading, last)])


def apply_table(table, values):
    return jnp.dot(
        table, values, precision=lax.Precision.HIGHEST, preferred_element_type=jnp.float32
    )


def spectra(cos_table, sin_table, real_part, imag_part):
    out_real = apply_table(cos_table, real_part) + apply_table(sin_table, imag_part)
    out_imag = apply_table(cos_table, imag_part) - apply_table(sin_table, real_part)
    return (out_real, out_imag)


def to_slots(cos_table, sin_table, real_part, imag_part):
    factor = 1.0 / cos_table.shape[0]
    cos_back = cos_table.T
    sin_back = sin_table.T
    out_real = (apply_table(cos_back, real_part) - apply_table(sin_back, imag_part)) * factor
    out_imag = (apply_table(cos_back, imag_part) + apply_table(sin_back, real_part)) * factor
    return (out_real, out_imag)


def sandwich(matrix, polar):
    left = jnp.einsum("ij,cejk->ceik", matrix, polar, preferred_element_type=jnp.float32).astype(
        jnp.bfloat16
    )
    return jnp.einsum("ceij,kj->ceik", left, matrix, preferred_element_type=jnp.float32)


def sandwich_t(matrix, polar):
    left = jnp.einsum("ji,cejk->ceik", matrix, polar, preferred_element_type=jnp.float32).astype(
        jnp.bfloat16
    )
    return jnp.einsum("ceij,jk->ceik", left, matrix, preferred_element_type=jnp.float32)


def shards(green, v_diag, v_low, energy_slot):
    energies = energy_slot.shape[0]
    period = 2 * energies
    frequency = jnp.arange(period, dtype=jnp.int32)
    phases = frequency[:, None] * energy_slot[None, :] % period
    angles = phases.astype(jnp.float32) * (2.0 * math.pi / period)
    cos_table = jnp.cos(angles)
    sin_table = jnp.sin(angles)
    scaling = energies ** (-0.5)
    arrived = lax.all_to_all(green[:, :, 0], "energy", split_axis=2, concat_axis=1, tiled=True)
    row_count = arrived.shape[2]
    col_count = arrived.shape[3]
    flattened = arrived.reshape((4, energies, row_count * col_count)).astype(jnp.float32)
    lesser_re, lesser_im = spectra(cos_table, sin_table, flattened[0], flattened[1])
    greater_re, greater_im = spectra(cos_table, sin_table, flattened[2], flattened[3])
    cross_re = lesser_re * greater_re + lesser_im * greater_im
    cross_im = lesser_im * greater_re - lesser_re * greater_im
    corr_re, corr_im = to_slots(cos_table, sin_table, cross_re, cross_im)
    polar_slot = (
        jnp.stack([corr_im * scaling, -corr_re * scaling])
        .reshape((2, energies, row_count, col_count))
        .astype(jnp.bfloat16)
    )
    polar = lax.all_to_all(polar_slot, "energy", split_axis=1, concat_axis=2, tiled=True)
    diagonal = v_diag[0]
    lower = v_low[0]
    own_term = sandwich(diagonal, polar)
    below = shifted(polar, "space", 1)
    handed = sandwich_t(lower, polar).astype(jnp.bfloat16)
    received = shifted(handed, "space", -1)
    total = own_term + sandwich(lower, below) + received.astype(jnp.float32)
    screened = total.astype(jnp.bfloat16)
    screened_rows = lax.all_to_all(screened, "energy", split_axis=2, concat_axis=1, tiled=True)
    weights = screened_rows.reshape((2, energies, row_count * col_count)).astype(jnp.float32)
    weight_re, weight_im = spectra(cos_table, sin_table, weights[0], weights[1])
    joint_re = lesser_re * weight_re - lesser_im * weight_im
    joint_im = lesser_re * weight_im + lesser_im * weight_re
    conv_re, conv_im = to_slots(cos_table, sin_table, joint_re, joint_im)
    sigma = (
        jnp.stack([-conv_im * scaling, conv_re * scaling])
        .reshape((2, energies, row_count, col_count))
        .astype(jnp.bfloat16)
    )
    return sigma[:, :, None]


def solution(mesh):
    in_specs = (
        P(None, "energy", "space", None, None),
        P("space", None, None),
        P("space", None, None),
        P(),
    )
    out_specs = P(None, None, "space", "energy", None)
    return jax.shard_map(shards, mesh=mesh, in_specs=in_specs, out_specs=out_specs, check_vma=False)
```

profile of v0, /device:TPU:24, one launch (start us, length us, event | category | flops | bytes accessed | tf_op | source)
XLA Modules:
  0.0 103.2 jit_solution(476986298993754648)
XLA Ops:
  0.0 2.2 %copy.56 = bf16[4,1,1,384,384]{4,0,3,2,1:T(4,128)(2,1)S(1)} copy(bf16[4,1,1,384,384]{4,3,2,1,0:T(8,128)(2,1)} %param.4) | data formatting | bytes 2359296 | tf_op args[0]
  2.2 20.3 %all_to_all.30 = bf16[4,1,384,384]{3,0,1,2:T(4,128)(2,1)S(1)} all-to-all(bf16[4,1,384,384]{3,0,1,2:T(4,128)(2,1)S(1)} %bitcast.85), channel_id=1, replica_groups=mesh['energy'=8,'space'=4] {'energy'}, dimensions={2} | all-to-all | bytes 2359296 | tf_op jit(solution)/shard_map/all_to_all | solution.py:58
  22.5 7.5 %slice_reduce_fusion.3 = (bf16[384,384]{1,0:T(8,128)(2,1)S(1)}, bf16[384,384]{1,0:T(8,128)(2,1)S(1)}, bf16[384,384]{1,0:T(8,128)(2,1)S(1)}, bf16[384,384]{1,0:T(8,128)(2,1)S(1)}) fusion(bf16[4,1,384,384]{3,0,1,2:T(4,128)(2,1)S(1)} %all_to_all.30), kind=kLoop, calls=%fused_computation.42 | loop fusion | bytes 2359296 | tf_op jit(solution)/shard_map/slice | solution.py:63
  30.7 0.7 fusion.52
  31.4 0.7 fusion.50
  32.0 0.7 convolution_subtract_fusion.2
  34.0 0.7 convolution_subtract_fusion.1
  34.7 0.7 convolution_add_fusion.1
  35.4 2.1 %multiply_subtract_fusion.1 = (f32[16,18432]{1,0:T(8,128)S(1)}, f32[16,18432]{1,0:T(8,128)S(1)}, f32[16,18432]{1,0:T(8,128)}) fusion(f32[16,18432]{1,0:T(8,128)S(1)} %convolution_subtract_fusion.1, f32[16,18432]{1,0:T(8,128)S(1)} %convolution_subtract_fusion.2, f32[16,18432]{1,0:T(8,128)S(1)} %convolution_add_fusion.1, f32[16,18432]{1,0:T(8,128)S(1)} %fusion.52, ...), kind=kOutput, calls=%fused_computation.38 | convolution fusion | flops 30377728 | bytes 8552480 | tf_op jit(solution)/shard_map/dot_general | solution.py:15
  37.4 0.7 fusion.44
  38.2 0.7 fusion.42
  38.9 0.8 fusion.8
  39.7 0.8 fusion.9
  40.6 12.8 %all_to_all.31 = bf16[2,8,48,384]{3,2,0,1:T(8,128)(2,1)S(1)} all-to-all(bf16[2,8,48,384]{3,2,0,1:T(8,128)(2,1)S(1)} %pad_maximum_fusion), channel_id=1, replica_groups=mesh['energy'=8,'space'=4] {'energy'}, dimensions={1} | all-to-all | bytes 1179648 | tf_op jit(solution)/shard_map/all_to_all | solution.py:72
  53.5 1.1 %copy.43 = bf16[2,1,384,384]{2,3,0,1:T(8,128)(2,1)} copy(bf16[2,1,384,384]{3,2,0,1:T(8,128)(2,1)S(1)} %bitcast.82) | data formatting | bytes 1179648 | tf_op jit(solution)/shard_map/all_to_all | solution.py:72
  54.6 1.9 %fusion.17 = bf16[2,1,384,384]{3,2,0,1:T(8,128)(2,1)} fusion(bf16[2,384,384]{2,1,0:T(8,128)(2,1)S(1)} %bitcast.83, bf16[1,384,384]{2,1,0:T(8,128)(2,1)S(1)} %copy-done), kind=kOutput, calls=%fused_computation.32 | convolution fusion | flops 453574656 | bytes 1474560 | tf_op jit(solution)/shard_map/ceij,jk->ceik/dot_general | solution.py:46
  56.5 3.2 %collective-permute-start.1 = (bf16[2,1,384,384]{3,2,0,1:T(8,128)(2,1)}, bf16[2,1,384,384]{3,2,0,1:T(8,128)(2,1)}, u32[]{:S(2)}, u32[]{:S(2)}) collective-permute-start(bf16[2,1,384,384]{3,2,0,1:T(8,128)(2,1)} %fusion.17), channel_id=1, source_target_pairs={{1,0},{2,1},{3,2},{5,4},{6,5},{7,6},{9,8},{10,9},{11,10},{13,12},{... | collective-permute-start | bytes 1769480 | tf_op jit(solution)/shard_map/ppermute | solution.py:11
  59.7 1.5 %collective-permute-start = (bf16[2,1,384,384]{2,3,0,1:T(8,128)(2,1)}, bf16[2,1,384,384]{2,3,0,1:T(8,128)(2,1)}, u32[]{:S(2)}, u32[]{:S(2)}) collective-permute-start(bf16[2,1,384,384]{2,3,0,1:T(8,128)(2,1)} %copy.43), channel_id=1, source_target_pairs={{0,1},{1,2},{2,3},{4,5},{5,6},{6,7},{8,9},{9,10},{10,11},{12,13},{... | collective-permute-start | bytes 1769480 | tf_op jit(solution)/shard_map/ppermute | solution.py:11
  61.2 1.1 %fusion.14 = f32[2,384,384]{2,1,0:T(8,128)S(1)} fusion(bf16[2,384,384]{2,1,0:T(8,128)(2,1)S(1)} %bitcast.84, bf16[1,384,384]{2,1,0:T(8,128)(2,1)S(1)} %copy-done.2), kind=kOutput, calls=%fused_computation.29 | convolution fusion | flops 453279744 | bytes 2064384 | tf_op jit(solution)/shard_map/ceij,kj->ceik/dot_general | solution.py:39
  62.3 9.4 %collective-permute-done.1 = bf16[2,1,384,384]{3,2,0,1:T(8,128)(2,1)} collective-permute-done((bf16[2,1,384,384]{3,2,0,1:T(8,128)(2,1)}, bf16[2,1,384,384]{3,2,0,1:T(8,128)(2,1)}, u32[]{:S(2)}, u32[]{:S(2)}) %collective-permute-start.1) | collective-permute-done | bytes 589856 | tf_op jit(solution)/shard_map/ppermute | solution.py:11
  71.6 5.0 %collective-permute-done = bf16[2,1,384,384]{2,3,0,1:T(8,128)(2,1)} collective-permute-done((bf16[2,1,384,384]{2,3,0,1:T(8,128)(2,1)}, bf16[2,1,384,384]{2,3,0,1:T(8,128)(2,1)}, u32[]{:S(2)}, u32[]{:S(2)}) %collective-permute-start) | collective-permute-done | bytes 589856 | tf_op jit(solution)/shard_map/ppermute | solution.py:11
  76.6 2.3 %add_convert_fusion = bf16[2,1,384,384]{3,2,0,1:T(8,128)(2,1)S(1)} fusion(bf16[2,1,384,384]{3,2,0,1:T(8,128)(2,1)} %collective-permute-done.1, f32[2,384,384]{2,1,0:T(8,128)S(1)} %fusion.14, bf16[2,1,384,384]{2,3,0,1:T(8,128)(2,1)} %collective-permute-done, bf16[1,384,384]{2,1,0:T(8,128)(2,1)S(1)} %copy-done), kind=kOutput, calls=%fused_computation.36 | convolution fusion | flops 454459392 | bytes 3244032 | tf_op jit(solution)/shard_map/ceij,kj->ceik/dot_general | solution.py:39
  79.5 12.8 %all_to_all.32 = bf16[2,1,384,384]{3,0,1,2:T(2,128)(2,1)S(1)} all-to-all(bf16[2,1,384,384]{3,0,1,2:T(2,128)(2,1)S(1)} %copy.47), channel_id=1, replica_groups=mesh['energy'=8,'space'=4] {'energy'}, dimensions={2} | all-to-all | bytes 1179648 | tf_op jit(solution)/shard_map/all_to_all | solution.py:81
  92.3 2.9 %slice_reduce_fusion = (bf16[384,384]{1,0:T(8,128)(2,1)S(1)}, bf16[384,384]{1,0:T(8,128)(2,1)S(1)}) fusion(bf16[2,1,384,384]{3,0,1,2:T(2,128)(2,1)S(1)} %all_to_all.32), kind=kLoop, calls=%fused_computation.39 | loop fusion | bytes 1179648 | tf_op jit(solution)/shard_map/slice | solution.py:83
  96.2 0.7 fusion.38
  96.9 0.7 convolution_subtract_fusion
  98.1 1.0 %multiply_add_fusion = (f32[16,18432]{1,0:T(8,128)S(1)}, f32[16,18432]{1,0:T(8,128)S(1)}) fusion(f32[16,18432]{1,0:T(8,128)S(1)} %convolution_subtract_fusion.2, f32[16,18432]{1,0:T(8,128)S(1)} %copy-done.1, f32[16,18432]{1,0:T(8,128)S(1)} %convolution_subtract_fusion, f32[16,18432]{1,0:T(8,128)S(1)} %fusion.38, bf16[8,18432]{1,0:T(8,128)(2,1)S(1)} %squeeze.34, ...), kind=kOutput, calls=%fused_computation.35 | convolution fusion | flops 30377728 | bytes 7372832 | tf_op jit(solution)/shard_map/dot_general | solution.py:15
  99.2 0.7 fusion.36
  99.9 0.7 fusion.34
  100.7 0.8 fusion.10
  101.5 0.7 fusion.11
  102.3 0.9 pad_maximum_fusion.1
  (24 shorter events, 4.3 us)
Async XLA Ops:
  0.0 54.6 %copy-start = (bf16[1,384,384]{2,1,0:T(8,128)(2,1)S(1)}, bf16[1,384,384]{2,1,0:T(8,128)(2,1)}, u32[]{:S(2)}) copy-start(bf16[1,384,384]{2,1,0:T(8,128)(2,1)} %param.6) | copy-start | bytes 884740
  30.0 0.7 copy-start.3
  54.6 6.6 %copy-start.2 = (bf16[1,384,384]{2,1,0:T(8,128)(2,1)S(1)}, bf16[1,384,384]{2,1,0:T(8,128)(2,1)}, u32[]{:S(2)}) copy-start(bf16[1,384,384]{2,1,0:T(8,128)(2,1)} %param.5) | copy-start | bytes 884740
  56.5 15.2 %collective-permute-start.1 = (bf16[2,1,384,384]{3,2,0,1:T(8,128)(2,1)}, bf16[2,1,384,384]{3,2,0,1:T(8,128)(2,1)}, u32[]{:S(2)}, u32[]{:S(2)}) collective-permute-start(bf16[2,1,384,384]{3,2,0,1:T(8,128)(2,1)} %fusion.17), channel_id=1, source_target_pairs={{1,0},{2,1},{3,2},{5,4},{6,5},{7,6},{9,8},{10,9},{11,10},{13,12},{... | collective-permute-start | bytes 1769480 | tf_op jit(solution)/shard_map/ppermute | solution.py:11
  59.7 16.9 %collective-permute-start = (bf16[2,1,384,384]{2,3,0,1:T(8,128)(2,1)}, bf16[2,1,384,384]{2,3,0,1:T(8,128)(2,1)}, u32[]{:S(2)}, u32[]{:S(2)}) collective-permute-start(bf16[2,1,384,384]{2,3,0,1:T(8,128)(2,1)} %copy.43), channel_id=1, source_target_pairs={{0,1},{1,2},{2,3},{4,5},{5,6},{6,7},{8,9},{9,10},{10,11},{12,13},{... | collective-permute-start | bytes 1769480 | tf_op jit(solution)/shard_map/ppermute | solution.py:11
  96.9 1.3 %copy-start.1 = (f32[16,18432]{1,0:T(8,128)S(1)}, f32[16,18432]{1,0:T(8,128)}, u32[]{:S(2)}) copy-start(f32[16,18432]{1,0:T(8,128)} %get-tuple-element.15) | copy-start | bytes 3538948
where the time goes:
time: 104 us; the launch traced here: 103 us
  blocking collectives  45.9 us (44%)
  matrix products  20.9 us (20%)
  local copies, waits for them, and re-layouts  16.1 us (15%)
  waiting for transfers between devices  14.3 us (14%)
  starting transfers between devices  4.7 us (5%)
    all_to_all x1, blocking collectives, shards(): lax.all_to_all(green[:, :, 0], 'energy', split_axis=2, concat_axis=1, til...  20.3 us
    dot_general x20, matrix products, apply_table(): jnp.dot(table, values, precision=lax.Precision.HIGHEST, preferred_element...  15.7 us
    ppermute x2, waiting for transfers between devices, shifted(): lax.ppermute(value, axis, [(source, source + steps) for source in range(l...  14.3 us
    all_to_all x1, blocking collectives, shards(): lax.all_to_all(polar_slot, 'energy', split_axis=1, concat_axis=2, tiled=T...  12.8 us
    all_to_all x1, blocking collectives, shards(): lax.all_to_all(screened, 'energy', split_axis=2, concat_axis=1, tiled=True)  12.8 us
    slice x1, local copies, waits for them, and re-layouts, shards(): flattened[2]  7.53 us
    ppermute x2, starting transfers between devices, shifted(): lax.ppermute(value, axis, [(source, source + steps) for source in range(l...  4.7 us
    dot_general x2, matrix products, sandwich(): jnp.einsum('ceij,kj->ceik', left, matrix, preferred_element_type=jnp.floa...  3.35 us
  transfers between devices with their start and end apart: 2, of which 2 were waited for; matrix products, arithmetic and copies ran while one was open for 1% of the time, Pallas kernels for 0%

commit v1 on v0

--- a/solution.py
+++ b/solution.py
@@ -1,8 +1,37 @@
+import functools
 import math
 import jax
 import jax.numpy as jnp
 from jax import lax
 from jax.sharding import PartitionSpec as P
+
+
+def manage_signs_on(chunk, along_dim, inputs):
+    small, y_new = (chunk.shape[:along_dim], chunk.shape[along_dim + 1 :])
+    row_out = jnp.moveaxis(chunk.reshape(*small, inputs, -1, *y_new), along_dim, 0)
+    return row_out
+
+
+def divide_sheet_up(original, which_dim):
+    e_next = list(original.shape[1:])
+    e_next[which_dim] *= original.shape[0]
+    p_next = jnp.moveaxis(original, 0, which_dim).reshape(e_next)
+    return p_next
+
+
+def treat_views(arr_in, group_axis, load, content):
+    ready, local_part = (lax.psum(1, group_axis), lax.axis_index(group_axis))
+    latest = manage_signs_on(arr_in, load, ready)
+    rack = [latest[local_part]]
+    for idx in range(1, ready):
+        r_now = latest[local_part ^ idx]
+        rack.append(lax.ppermute(r_now, group_axis, [(nth, nth ^ idx) for nth in range(ready)]))
+    latest = jnp.stack(rack)[local_part ^ jnp.arange(ready)]
+    w2 = divide_sheet_up(latest, content)
+    return w2
+
+
+feed_tasks_up = functools.partial(treat_views, group_axis="energy", load=2, content=1)
 
 
 def shifted(value, axis, steps):
@@ -55,7 +84,7 @@
     cos_table = jnp.cos(angles)
     sin_table = jnp.sin(angles)
     scaling = energies ** (-0.5)
-    arrived = lax.all_to_all(green[:, :, 0], "energy", split_axis=2, concat_axis=1, tiled=True)
+    arrived = feed_tasks_up(green[:, :, 0])
     row_count = arrived.shape[2]
     col_count = arrived.shape[3]
     flattened = arrived.reshape((4, energies, row_count * col_count)).astype(jnp.float32)

time: 104 us -> 95.6 us (0.919)
  blocking collectives: 45.9 us -> 25.8 us
  waiting for transfers between devices: 14.3 us -> 25.6 us
  starting transfers between devices: 4.7 us -> 11.8 us
  local copies, waits for them, and re-layouts: 16.1 us -> 9.77 us
    all_to_all x1 -> x0, blocking collectives: 20.3 us -> none  [shards(): lax.all_to_all(green[:, :, 0], 'energy', split_axis=2, concat_axis=1, til...]
    ppermute x0 -> x7, waiting for transfers between devices: none -> 11.3 us  [treat_views(): lax.ppermute(r_now, group_axis, [(nth, nth ^ idx) for nth in range(ready)])]
    slice x1 -> x0, local copies, waits for them, and re-layouts: 7.53 us -> none  [shards(): flattened[2]]
    ppermute x0 -> x7, starting transfers between devices: none -> 7.14 us  [treat_views(): lax.ppermute(r_now, group_axis, [(nth, nth ^ idx) for nth in range(ready)])]
    unnamed x9 -> x20, local copies, waits for them, and re-layouts: 2.88 us -> 2.42 us
  transfers between devices with their start and end apart: 2 -> 9, of which waited for: 2 -> 5; matrix products, arithmetic and copies ran while one was open for 1% -> 2% of each run, Pallas kernels for 0% -> 0%
where the time goes in v1:
time: 95.6 us; the launch traced here: 95.3 us
  blocking collectives  25.8 us (27%)
  waiting for transfers between devices  25.6 us (27%)
  matrix products  21 us (22%)
  starting transfers between devices  11.8 us (12%)
  local copies, waits for them, and re-layouts  9.77 us (10%)
  other arithmetic  0.97 us (1%)
    dot_general x20, matrix products, apply_table(): jnp.dot(table, values, precision=lax.Precision.HIGHEST, preferred_element...  15.7 us
    ppermute x2, waiting for transfers between devices, shifted(): lax.ppermute(value, axis, [(source, source + steps) for source in range(l...  14.4 us
    all_to_all x1, blocking collectives, shards(): lax.all_to_all(polar_slot, 'energy', split_axis=1, concat_axis=2, tiled=T...  13 us
    all_to_all x1, blocking collectives, shards(): lax.all_to_all(screened, 'energy', split_axis=2, concat_axis=1, tiled=True)  12.8 us
    ppermute x7, waiting for transfers between devices, treat_views(): lax.ppermute(r_now, group_axis, [(nth, nth ^ idx) for nth in range(ready)])  11.3 us
    ppermute x7, starting transfers between devices, treat_views(): lax.ppermute(r_now, group_axis, [(nth, nth ^ idx) for nth in range(ready)])  7.14 us
    ppermute x2, starting transfers between devices, shifted(): lax.ppermute(value, axis, [(source, source + steps) for source in range(l...  4.63 us
    dot_general x2, matrix products, sandwich(): jnp.einsum('ceij,kj->ceik', left, matrix, preferred_element_type=jnp.floa...  3.34 us
  transfers between devices with their start and end apart: 9, of which 5 were waited for; matrix products, arithmetic and copies ran while one was open for 2% of the time, Pallas kernels for 0%

profile of v1, /device:TPU:24, one launch (start us, length us, event | category | flops | bytes accessed | tf_op | source)
XLA Modules:
  0.0 95.3 jit_solution(13473231912697713155)
XLA Ops:
  0.0 1.4 %dynamic-slice_bitcast_fusion = (bf16[4,1,48,384]{3,2,0,1:T(8,128)(2,1)S(1)}, bf16[4,1,48,384]{3,2,0,1:T(8,128)(2,1)S(1)}, bf16[4,1,48,384]{3,2,0,1:T(8,128)(2,1...) fusion(bf16[4,1,8,48,384]{4,3,2,0,1:T(8,128)(2,1)} %bitcast.153, ...), kind=kLoop, calls=%fused_computation.59 | loop fusion | bytes 2064412 | tf_op jit(solution)/shard_map/squeeze | solution.py:27
  1.4 2.0 %collective-permute-start.6 = (bf16[4,1,48,384]{3,2,0,1:T(8,128)(2,1)S(1)}, bf16[4,1,48,384]{3,2,0,1:T(8,128)(2,1)S(1)}, u32[]{:S(2)}, u32[]{:S(2)}) collective-permute-start(bf16[4,1,48,384]{3,2,0,1:T(8,128)(2,1)S(1)} %get-tuple-element.15), channel_id=1, source_target_pairs={{0,28},{4,24},{8,20},{12,16},{16,12},{20,8},{24,4},{28,0},{1,29},{... | collective-permute-start | bytes 442376 | tf_op jit(solution)/shard_map/ppermute | solution.py:28
  4.0 1.4 %collective-permute-start.4 = (bf16[4,1,48,384]{3,2,0,1:T(8,128)(2,1)S(1)}, bf16[4,1,48,384]{3,2,0,1:T(8,128)(2,1)S(1)}, u32[]{:S(2)}, u32[]{:S(2)}) collective-permute-start(bf16[4,1,48,384]{3,2,0,1:T(8,128)(2,1)S(1)} %get-tuple-element.17), channel_id=1, source_target_pairs={{0,20},{4,16},{8,28},{12,24},{16,4},{20,0},{24,12},{28,8},{1,21},{... | collective-permute-start | bytes 442376 | tf_op jit(solution)/shard_map/ppermute | solution.py:28
  5.9 0.9 bitcast_dynamic-update-slice_fusion.7
  7.3 1.5 %collective-permute-start.1 = (bf16[4,1,48,384]{3,2,0,1:T(8,128)(2,1)S(1)}, bf16[4,1,48,384]{3,2,0,1:T(8,128)(2,1)S(1)}, u32[]{:S(2)}, u32[]{:S(2)}) collective-permute-start(bf16[4,1,48,384]{3,2,0,1:T(8,128)(2,1)S(1)} %get-tuple-element.20), channel_id=1, source_target_pairs={{0,8},{4,12},{8,0},{12,4},{16,24},{20,28},{24,16},{28,20},{1,9},{5... | collective-permute-start | bytes 442376 | tf_op jit(solution)/shard_map/ppermute | solution.py:28
  8.8 6.2 %collective-permute-done.1 = bf16[4,1,48,384]{3,2,0,1:T(8,128)(2,1)S(1)} collective-permute-done((bf16[4,1,48,384]{3,2,0,1:T(8,128)(2,1)S(1)}, bf16[4,1,48,384]{3,2,0,1:T(8,128)(2,1)S(1)}, u32[]{:S(2)}, u32[]{:S(2)}) %collective-permute-start.1) | collective-permute-done | bytes 147488 | tf_op jit(solution)/shard_map/ppermute | solution.py:28
  15.0 1.2 %collective-permute-start.2 = (bf16[4,1,48,384]{3,2,0,1:T(8,128)(2,1)S(1)}, bf16[4,1,48,384]{3,2,0,1:T(8,128)(2,1)S(1)}, u32[]{:S(2)}, u32[]{:S(2)}) collective-permute-start(bf16[4,1,48,384]{3,2,0,1:T(8,128)(2,1)S(1)} %get-tuple-element.19), channel_id=1, source_target_pairs={{0,12},{4,8},{8,4},{12,0},{16,28},{20,24},{24,20},{28,16},{1,13},{... | collective-permute-start | bytes 442376 | tf_op jit(solution)/shard_map/ppermute | solution.py:28
  16.2 4.6 %collective-permute-done.2 = bf16[4,1,48,384]{3,2,0,1:T(8,128)(2,1)S(1)} collective-permute-done((bf16[4,1,48,384]{3,2,0,1:T(8,128)(2,1)S(1)}, bf16[4,1,48,384]{3,2,0,1:T(8,128)(2,1)S(1)}, u32[]{:S(2)}, u32[]{:S(2)}) %collective-permute-start.2) | collective-permute-done | bytes 147488 | tf_op jit(solution)/shard_map/ppermute | solution.py:28
  21.1 0.8 gather_fusion
  26.0 0.7 convolution_subtract_fusion.1
  27.3 2.1 %multiply_subtract_fusion.1 = (f32[16,18432]{1,0:T(8,128)S(1)}, f32[16,18432]{1,0:T(8,128)S(1)}, f32[16,18432]{1,0:T(8,128)}) fusion(f32[16,18432]{1,0:T(8,128)S(1)} %convolution_subtract_fusion.1, f32[16,18432]{1,0:T(8,128)S(1)} %convolution_subtract_fusion.2, f32[16,18432]{1,0:T(8,128)S(1)} %convolution_add_fusion.1, f32[16,18432]{1,0:T(8,128)S(1)} %fusion.52, ...), kind=kOutput, calls=%fused_computation.38 | convolution fusion | flops 30377728 | bytes 8552480 | tf_op jit(solution)/shard_map/dot_general | solution.py:44
  29.4 0.7 fusion.44
  30.2 0.7 fusion.42
  30.9 0.7 fusion.8
  31.7 0.8 fusion.9
  32.6 13.0 %all_to_all.21 = bf16[2,8,48,384]{3,2,0,1:T(8,128)(2,1)S(1)} all-to-all(bf16[2,8,48,384]{3,2,0,1:T(8,128)(2,1)S(1)} %pad_maximum_fusion), channel_id=1, replica_groups=mesh['energy'=8,'space'=4] {'energy'}, dimensions={1} | all-to-all | bytes 1179648 | tf_op jit(solution)/shard_map/all_to_all | solution.py:101
  45.7 1.1 %copy.41 = bf16[2,1,384,384]{2,3,0,1:T(8,128)(2,1)} copy(bf16[2,1,384,384]{3,2,0,1:T(8,128)(2,1)S(1)} %bitcast.136) | data formatting | bytes 1179648 | tf_op jit(solution)/shard_map/all_to_all | solution.py:101
  46.7 1.9 %fusion.17 = bf16[2,1,384,384]{3,2,0,1:T(8,128)(2,1)} fusion(bf16[2,384,384]{2,1,0:T(8,128)(2,1)S(1)} %bitcast.137, bf16[1,384,384]{2,1,0:T(8,128)(2,1)S(1)} %copy-done), kind=kOutput, calls=%fused_computation.33 | convolution fusion | flops 453574656 | bytes 1474560 | tf_op jit(solution)/shard_map/ceij,jk->ceik/dot_general | solution.py:75
  48.6 3.2 %collective-permute-start.8 = (bf16[2,1,384,384]{3,2,0,1:T(8,128)(2,1)}, bf16[2,1,384,384]{3,2,0,1:T(8,128)(2,1)}, u32[]{:S(2)}, u32[]{:S(2)}) collective-permute-start(bf16[2,1,384,384]{3,2,0,1:T(8,128)(2,1)} %fusion.17), channel_id=1, source_target_pairs={{1,0},{2,1},{3,2},{5,4},{6,5},{7,6},{9,8},{10,9},{11,10},{13,12},{... | collective-permute-start | bytes 1769480 | tf_op jit(solution)/shard_map/ppermute | solution.py:40
  51.8 1.5 %collective-permute-start.7 = (bf16[2,1,384,384]{2,3,0,1:T(8,128)(2,1)}, bf16[2,1,384,384]{2,3,0,1:T(8,128)(2,1)}, u32[]{:S(2)}, u32[]{:S(2)}) collective-permute-start(bf16[2,1,384,384]{2,3,0,1:T(8,128)(2,1)} %copy.41), channel_id=1, source_target_pairs={{0,1},{1,2},{2,3},{4,5},{5,6},{6,7},{8,9},{9,10},{10,11},{12,13},{... | collective-permute-start | bytes 1769480 | tf_op jit(solution)/shard_map/ppermute | solution.py:40
  53.3 1.1 %fusion.14 = f32[2,384,384]{2,1,0:T(8,128)S(1)} fusion(bf16[2,384,384]{2,1,0:T(8,128)(2,1)S(1)} %bitcast.138, bf16[1,384,384]{2,1,0:T(8,128)(2,1)S(1)} %copy-done.2), kind=kOutput, calls=%fused_computation.30 | convolution fusion | flops 453279744 | bytes 2064384 | tf_op jit(solution)/shard_map/ceij,kj->ceik/dot_general | solution.py:68
  54.3 9.4 %collective-permute-done.8 = bf16[2,1,384,384]{3,2,0,1:T(8,128)(2,1)} collective-permute-done((bf16[2,1,384,384]{3,2,0,1:T(8,128)(2,1)}, bf16[2,1,384,384]{3,2,0,1:T(8,128)(2,1)}, u32[]{:S(2)}, u32[]{:S(2)}) %collective-permute-start.8) | collective-permute-done | bytes 589856 | tf_op jit(solution)/shard_map/ppermute | solution.py:40
  63.8 4.9 %collective-permute-done.7 = bf16[2,1,384,384]{2,3,0,1:T(8,128)(2,1)} collective-permute-done((bf16[2,1,384,384]{2,3,0,1:T(8,128)(2,1)}, bf16[2,1,384,384]{2,3,0,1:T(8,128)(2,1)}, u32[]{:S(2)}, u32[]{:S(2)}) %collective-permute-start.7) | collective-permute-done | bytes 589856 | tf_op jit(solution)/shard_map/ppermute | solution.py:40
  68.7 2.3 %add_convert_fusion = bf16[2,1,384,384]{3,2,0,1:T(8,128)(2,1)S(1)} fusion(bf16[2,1,384,384]{3,2,0,1:T(8,128)(2,1)} %collective-permute-done.8, f32[2,384,384]{2,1,0:T(8,128)S(1)} %fusion.14, bf16[2,1,384,384]{2,3,0,1:T(8,128)(2,1)} %collective-permute-done.7, bf16[1,384,384]{2,1,0:T(8,128)(2,1)S(1)} %copy-done), kind=kOutput, calls=%fused_computation.36 | convolution fusion | flops 454459392 | bytes 3244032 | tf_op jit(solution)/shard_map/ceij,kj->ceik/dot_general | solution.py:68
  71.6 12.8 %all_to_all.22 = bf16[2,1,384,384]{3,0,1,2:T(2,128)(2,1)S(1)} all-to-all(bf16[2,1,384,384]{3,0,1,2:T(2,128)(2,1)S(1)} %copy.45), channel_id=1, replica_groups=mesh['energy'=8,'space'=4] {'energy'}, dimensions={2} | all-to-all | bytes 1179648 | tf_op jit(solution)/shard_map/all_to_all | solution.py:110
  84.4 2.9 %slice_reduce_fusion = (bf16[384,384]{1,0:T(8,128)(2,1)S(1)}, bf16[384,384]{1,0:T(8,128)(2,1)S(1)}) fusion(bf16[2,1,384,384]{3,0,1,2:T(2,128)(2,1)S(1)} %all_to_all.22), kind=kLoop, calls=%fused_computation.39 | loop fusion | bytes 1179648 | tf_op jit(solution)/shard_map/slice | solution.py:112
  90.2 1.0 %multiply_add_fusion = (f32[16,18432]{1,0:T(8,128)S(1)}, f32[16,18432]{1,0:T(8,128)S(1)}) fusion(f32[16,18432]{1,0:T(8,128)S(1)} %convolution_subtract_fusion.2, f32[16,18432]{1,0:T(8,128)S(1)} %copy-done.1, f32[16,18432]{1,0:T(8,128)S(1)} %convolution_subtract_fusion, f32[16,18432]{1,0:T(8,128)S(1)} %fusion.38, bf16[8,18432]{1,0:T(8,128)(2,1)S(1)} %squeeze.58, ...), kind=kOutput, calls=%fused_computation.35 | convolution fusion | flops 30377728 | bytes 7372832 | tf_op jit(solution)/shard_map/dot_general | solution.py:44
  91.3 0.7 fusion.36
  92.0 0.7 fusion.34
  92.8 0.8 fusion.10
  93.6 0.7 fusion.11
  94.4 0.9 pad_maximum_fusion.1
  (48 shorter events, 10.2 us)
Async XLA Ops:
  0.0 46.7 %copy-start = (bf16[1,384,384]{2,1,0:T(8,128)(2,1)S(1)}, bf16[1,384,384]{2,1,0:T(8,128)(2,1)}, u32[]{:S(2)}) copy-start(bf16[1,384,384]{2,1,0:T(8,128)(2,1)} %param.6) | copy-start | bytes 884740
  1.4 19.6 %collective-permute-start.6 = (bf16[4,1,48,384]{3,2,0,1:T(8,128)(2,1)S(1)}, bf16[4,1,48,384]{3,2,0,1:T(8,128)(2,1)S(1)}, u32[]{:S(2)}, u32[]{:S(2)}) collective-permute-start(bf16[4,1,48,384]{3,2,0,1:T(8,128)(2,1)S(1)} %get-tuple-element.15), channel_id=1, source_target_pairs={{0,28},{4,24},{8,20},{12,16},{16,12},{20,8},{24,4},{28,0},{1,29},{... | collective-permute-start | bytes 442376 | tf_op jit(solution)/shard_map/ppermute | solution.py:28
  3.4 17.6 %collective-permute-start.5 = (bf16[4,1,48,384]{3,2,0,1:T(8,128)(2,1)S(1)}, bf16[4,1,48,384]{3,2,0,1:T(8,128)(2,1)S(1)}, u32[]{:S(2)}, u32[]{:S(2)}) collective-permute-start(bf16[4,1,48,384]{3,2,0,1:T(8,128)(2,1)S(1)} %get-tuple-element.16), channel_id=1, source_target_pairs={{0,24},{4,28},{8,16},{12,20},{16,8},{20,12},{24,0},{28,4},{1,25},{... | collective-permute-start | bytes 442376 | tf_op jit(solution)/shard_map/ppermute | solution.py:28
  4.0 16.9 %collective-permute-start.4 = (bf16[4,1,48,384]{3,2,0,1:T(8,128)(2,1)S(1)}, bf16[4,1,48,384]{3,2,0,1:T(8,128)(2,1)S(1)}, u32[]{:S(2)}, u32[]{:S(2)}) collective-permute-start(bf16[4,1,48,384]{3,2,0,1:T(8,128)(2,1)S(1)} %get-tuple-element.17), channel_id=1, source_target_pairs={{0,20},{4,16},{8,28},{12,24},{16,4},{20,0},{24,12},{28,8},{1,21},{... | collective-permute-start | bytes 442376 | tf_op jit(solution)/shard_map/ppermute | solution.py:28
  5.4 15.5 %collective-permute-start.3 = (bf16[4,1,48,384]{3,2,0,1:T(8,128)(2,1)S(1)}, bf16[4,1,48,384]{3,2,0,1:T(8,128)(2,1)S(1)}, u32[]{:S(2)}, u32[]{:S(2)}) collective-permute-start(bf16[4,1,48,384]{3,2,0,1:T(8,128)(2,1)S(1)} %get-tuple-element.18), channel_id=1, source_target_pairs={{0,16},{4,20},{8,24},{12,28},{16,0},{20,4},{24,8},{28,12},{1,17},{... | collective-permute-start | bytes 442376 | tf_op jit(solution)/shard_map/ppermute | solution.py:28
  5.9 1.4 %collective-permute-start = (bf16[4,1,48,384]{3,2,0,1:T(8,128)(2,1)S(1)}, bf16[4,1,48,384]{3,2,0,1:T(8,128)(2,1)S(1)}, u32[]{:S(2)}, u32[]{:S(2)}) collective-permute-start(bf16[4,1,48,384]{3,2,0,1:T(8,128)(2,1)S(1)} %get-tuple-element.21), channel_id=1, source_target_pairs={{0,4},{4,0},{8,12},{12,8},{16,20},{20,16},{24,28},{28,24},{1,5},{5... | collective-permute-start | bytes 442376 | tf_op jit(solution)/shard_map/ppermute | solution.py:28
  7.3 7.7 %collective-permute-start.1 = (bf16[4,1,48,384]{3,2,0,1:T(8,128)(2,1)S(1)}, bf16[4,1,48,384]{3,2,0,1:T(8,128)(2,1)S(1)}, u32[]{:S(2)}, u32[]{:S(2)}) collective-permute-start(bf16[4,1,48,384]{3,2,0,1:T(8,128)(2,1)S(1)} %get-tuple-element.20), channel_id=1, source_target_pairs={{0,8},{4,12},{8,0},{12,4},{16,24},{20,28},{24,16},{28,20},{1,9},{5... | collective-permute-start | bytes 442376 | tf_op jit(solution)/shard_map/ppermute | solution.py:28
  15.0 5.9 %collective-permute-start.2 = (bf16[4,1,48,384]{3,2,0,1:T(8,128)(2,1)S(1)}, bf16[4,1,48,384]{3,2,0,1:T(8,128)(2,1)S(1)}, u32[]{:S(2)}, u32[]{:S(2)}) collective-permute-start(bf16[4,1,48,384]{3,2,0,1:T(8,128)(2,1)S(1)} %get-tuple-element.19), channel_id=1, source_target_pairs={{0,12},{4,8},{8,4},{12,0},{16,28},{20,24},{24,20},{28,16},{1,13},{... | collective-permute-start | bytes 442376 | tf_op jit(solution)/shard_map/ppermute | solution.py:28
  22.0 0.7 copy-start.3
  46.7 6.5 %copy-start.2 = (bf16[1,384,384]{2,1,0:T(8,128)(2,1)S(1)}, bf16[1,384,384]{2,1,0:T(8,128)(2,1)}, u32[]{:S(2)}) copy-start(bf16[1,384,384]{2,1,0:T(8,128)(2,1)} %param.5) | copy-start | bytes 884740
  48.6 15.2 %collective-permute-start.8 = (bf16[2,1,384,384]{3,2,0,1:T(8,128)(2,1)}, bf16[2,1,384,384]{3,2,0,1:T(8,128)(2,1)}, u32[]{:S(2)}, u32[]{:S(2)}) collective-permute-start(bf16[2,1,384,384]{3,2,0,1:T(8,128)(2,1)} %fusion.17), channel_id=1, source_target_pairs={{1,0},{2,1},{3,2},{5,4},{6,5},{7,6},{9,8},{10,9},{11,10},{13,12},{... | collective-permute-start | bytes 1769480 | tf_op jit(solution)/shard_map/ppermute | solution.py:40
  51.8 16.9 %collective-permute-start.7 = (bf16[2,1,384,384]{2,3,0,1:T(8,128)(2,1)}, bf16[2,1,384,384]{2,3,0,1:T(8,128)(2,1)}, u32[]{:S(2)}, u32[]{:S(2)}) collective-permute-start(bf16[2,1,384,384]{2,3,0,1:T(8,128)(2,1)} %copy.41), channel_id=1, source_target_pairs={{0,1},{1,2},{2,3},{4,5},{5,6},{6,7},{8,9},{9,10},{10,11},{12,13},{... | collective-permute-start | bytes 1769480 | tf_op jit(solution)/shard_map/ppermute | solution.py:40
  89.0 1.3 %copy-start.1 = (f32[16,18432]{1,0:T(8,128)S(1)}, f32[16,18432]{1,0:T(8,128)}, u32[]{:S(2)}) copy-start(f32[16,18432]{1,0:T(8,128)} %get-tuple-element.22) | copy-start | bytes 3538948
